TPU v7x, 32 devices: a whole 2x2x4 slice. The times are simulated.
32 devices in a mesh: groups: 2 (over y), tm: 16 (over z, x, core).
Axes of the slice: x: 2, y: 2, z: 4, core: 2. Of those that a mesh axis runs over, the one named last changes fastest.
Arguments:
- start_frames: float32 [6, 4, 8, 256], P('groups'), parts along dimension 0, may hold values from -6 to 6
- plan: int32 [32], P(('groups', 'tm')), parts along dimension 0, may hold values from 0 to 999
- noise: float32 [16, 6, 4, 8, 256], P('tm', 'groups'), parts along dimension 1, may hold values from -6 to 6
- w_lift: float32 [3, 128], replicated, may hold values from -3.5 to 3.5
- w_time: float32 [128, 128], replicated, may hold values from -0.75 to 0.75
- spatial: float32 [2, 128, 9], replicated, may hold values from -2 to 2
- temporal: float32 [2, 128, 3], replicated, may hold values from -3.5 to 3.5
- w_point: bfloat16 [2, 128, 128], replicated, may hold values from -0.5 to 0.5
- w_out: float32 [128, 3], replicated, may hold values from -0.5 to 0.5
Outputs:
- trajectory: float32 [16, 6, 4, 8, 256], P('tm', 'groups'), parts along dimension 1
There are 2 independent parts, one for each index of `groups`. A program takes and returns all parts, laid end to end along the dimension named above; an argument that names none is the same for every part. Nothing has to cross between parts.
All inputs are finite; a program needn't handle non-finite values.
Results may differ from a plain program's by a relative error of at most 0.0023.
Values sent between devices are 32-bit elements; how exact they have to be, the bound alone decides.
A program may use at most 64 MiB of HBM per device.

v0:
```python
import functools
import math

import jax
import jax.numpy as jnp
from jax import lax
from jax.experimental import pallas as pl
from jax.experimental.pallas import tpu as pltpu
from jax.sharding import PartitionSpec as P

ITERS = 2
NOISE_SCALE = 2.0
MESH = pl.DeviceIdType.MESH
LANES = 128
HALO = 8
TILE_W = 32


def embedding(step_index, width):
    half_width = width // 2
    column = jnp.arange(half_width, dtype=jnp.float32)
    freqs = jnp.exp(-math.log(1000.0) * column / half_width)
    angles = step_index.astype(jnp.float32) * freqs
    return jnp.concatenate([jnp.sin(angles), jnp.cos(angles)])


def split_bf16(value):
    high = value.astype(jnp.bfloat16).astype(jnp.float32)
    return high, value - high


def kernel(
    n, share,
    start_ref, noise_ref, bias_ref, lift_ref, spatial_ref, temporal_ref, point_ref, wout_ref,
    out_ref,
    feat_a, feat_b, cols, lift_w, out_w, conv_w, both_w, pending, value, sent, got, sums, before,
    send_sem, recv_sem,
):
    channels, frames, rows, width = start_ref.shape
    hid = point_ref.shape[1]
    blocks = point_ref.shape[0]
    halves = width // LANES
    step_size = 1.0 / n
    me = lax.axis_index("tm")

    barrier = pltpu.get_barrier_semaphore()

    @pl.loop(1, n)
    def _(k):
        pl.semaphore_signal(
            barrier, inc=1, device_id={"tm": lax.rem(me + k, n)}, device_id_type=MESH
        )

    for feat in (feat_a, feat_b):
        zeros = jnp.zeros((frames * rows, HALO, hid), jnp.float32)
        feat[:, 0:HALO, :] = zeros
        feat[:, HALO + width : HALO + width + HALO, :] = zeros
    cols[...] = jnp.zeros_like(cols)
    cols[:, channels : channels + 1, :] = jnp.ones((frames * rows, 1, width), jnp.float32)
    lift_w[...] = jnp.zeros_like(lift_w)
    high, low = split_bf16(lift_ref[...])
    lift_w[0:channels, :] = high
    lift_w[8 : 8 + channels, :] = high
    lift_w[16 : 16 + channels, :] = low
    out_w[...] = jnp.zeros_like(out_w)
    high, low = split_bf16(wout_ref[...])
    out_w[0:channels, :] = high
    out_w[8 : 8 + channels, :] = low
    high, low = split_bf16(bias_ref[...])
    lift_w[channels : channels + 1, :] = high
    lift_w[16 + channels : 17 + channels, :] = low
    owned = frames * halves * rows // share
    for it in range(ITERS):
        if owned < n:
            sent[it, owned:n] = jnp.zeros((n - owned, channels, share, LANES), jnp.float32)

    spot = lax.broadcasted_iota(jnp.int32, (hid, hid), 0)
    diagonal = spot == lax.broadcasted_iota(jnp.int32, (hid, hid), 1)
    both_w[...] = jnp.zeros_like(both_w)
    for out in range(2):
        here = slice(out * hid, (out + 1) * hid)
        both_w[blocks, here, here] = jnp.full((hid, hid), 4.0 / hid, jnp.bfloat16)
        for block in range(blocks):
            both_w[block, here, here] = point_ref[block]
            for near in range(2):
                tap = near + 1 - out
                for col in range(3):
                    there = slice((3 * near + col) * hid, (3 * near + col + 1) * hid)
                    k = 3 * tap + col
                    weight = jnp.where(diagonal, spatial_ref[k, block : block + 1, :], 0.0)
                    conv_w[block, there, here] = weight.astype(jnp.bfloat16)

    def one_block(source, target, block):
        pairs = rows // 2
        span = pairs * TILE_W

        def convolve(tile):
            w0 = pl.multiple_of(tile * TILE_W, TILE_W)
            stacked = []
            for frame in range(frames):
                for pair in range(pairs):
                    near = [
                        source[
                            frame * rows + 2 * pair + k, pl.ds(w0 + HALO - 1 + c, TILE_W), :
                        ].astype(jnp.bfloat16)
                        for k in range(2)
                        for c in range(3)
                    ]
                    stacked.append(jnp.concatenate(near, axis=1))
            return jnp.dot(
                jnp.concatenate(stacked, axis=0), conv_w[block], preferred_element_type=jnp.float32
            )

        def finish(tile, conv):
            w0 = pl.multiple_of(tile * TILE_W, TILE_W)
            times = []
            for k in range(3):
                weight = temporal_ref[k, block : block + 1, :]
                times.append(jnp.concatenate([weight, weight], axis=1))

            def outer(frame, row, tap):
                parts = [
                    spatial_ref[3 * tap + c, block : block + 1, :]
                    * source[frame * rows + row, pl.ds(w0 + HALO - 1 + c, TILE_W), :]
                    for c in range(3)
                ]
                return parts[0] + parts[1] + parts[2]

            placed = []
            for frame in range(frames):
                for pair in range(pairs):
                    first = frame * span + pair * TILE_W
                    halves = []
                    for out, row, tap in ((0, 2 * pair - 1, 0), (1, 2 * pair + 2, 2)):
                        part = conv[first : first + TILE_W, out * hid : (out + 1) * hid]
                        if 0 <= row < rows:
                            part = part + outer(frame, row, tap)
                        halves.append(part)
                    placed.append(jnp.concatenate(halves, axis=1))
            placed = [
                jnp.concatenate(placed[frame * pairs : (frame + 1) * pairs], axis=0)
                for frame in range(frames)
            ]
            mixed = []
            for frame in range(frames):
                total = times[1] * placed[frame]
                if frame > 0:
                    total = total + times[0] * placed[frame - 1]
                if frame + 1 < frames:
                    total = total + times[2] * placed[frame + 1]
                mixed.append(total)
            flat = jnp.concatenate(mixed, axis=0)
            square = flat * flat
            scale = jnp.concatenate(
                [
                    jnp.broadcast_to(
                        lax.rsqrt(
                            jnp.sum(square[:, out * hid : (out + 1) * hid], axis=1, keepdims=True)
                            * (4.0 / hid)
                            + 4e-06
                        ),
                        (frames * span, hid),
                    )
                    for out in range(2)
                ],
                axis=1,
            )
            half = flat * scale
            normed = (half * jnp.tanh(half) + half).astype(jnp.bfloat16)
            update = jnp.dot(normed, both_w[block], preferred_element_type=jnp.float32)
            here = pl.ds(w0 + HALO, TILE_W)
            for frame in range(frames):
                for row in range(rows):
                    at = frame * rows + row
                    first = frame * span + (row // 2) * TILE_W
                    out = row % 2
                    part = update[first : first + TILE_W, out * hid : (out + 1) * hid]
                    fresh = source[at, here, :] + part
                    target[at, here, :] = fresh.astype(jnp.bfloat16).astype(jnp.float32)

        tiles = width // TILE_W
        pending[...] = convolve(0)

        @pl.loop(1, tiles)
        def _(tile):
            earlier = pending[...]
            pending[...] = convolve(tile)
            finish(tile - 1, earlier)

        finish(tiles - 1, pending[...])

    def network():
        lift_weights = lift_w[...].astype(jnp.bfloat16)

        @pl.loop(0, frames * rows, unroll=4)
        def _(at):
            state = cols[at]
            high, low = split_bf16(state)
            left = jnp.concatenate([high, low, high, jnp.zeros_like(high)], axis=0)
            lifted = lax.dot_general(
                left.astype(jnp.bfloat16), lift_weights, (((0,), (0,)), ((), ())),
                preferred_element_type=jnp.float32,
            )
            feat_a[at, HALO : HALO + width, :] = lifted.astype(jnp.bfloat16).astype(jnp.float32)

        refs = (feat_a, feat_b)
        for block in range(blocks):
            one_block(refs[block % 2], refs[(block + 1) % 2], block)
        last = refs[blocks % 2]
        out_weights = out_w[...].astype(jnp.bfloat16)
        for at in range(frames * rows):
            frame, row = divmod(at, rows)
            cells = last[at, HALO : HALO + width, :].astype(jnp.bfloat16)
            both = lax.dot_general(
                out_weights, cells, (((1,), (1,)), ((), ())), preferred_element_type=jnp.float32
            )
            result = both[0:8] + both[8:16]
            for channel in range(channels):
                for part in range(halves):
                    value[channel, frame * halves + part, row : row + 1, :] = result[
                        channel : channel + 1, part * LANES : (part + 1) * LANES
                    ]

    def groups(tile):
        size = share if rows % share == 0 else 1
        for first in range(0, rows, size):
            at = tile * rows + first
            yield at // share, at % share, first, size

    def copy_out(it, peer):
        return pltpu.make_async_remote_copy(
            src_ref=sent.at[it, peer], dst_ref=got.at[it, me],
            send_sem=send_sem.at[it, 0, peer], recv_sem=recv_sem.at[it, 0, me],
            device_id={"tm": peer}, device_id_type=MESH,
        )

    def copy_in(it, peer):
        return pltpu.make_async_remote_copy(
            src_ref=sent.at[it, peer], dst_ref=got.at[it, peer],
            send_sem=send_sem.at[it, 0, peer], recv_sem=recv_sem.at[it, 0, peer],
            device_id={"tm": peer}, device_id_type=MESH,
        )

    def back_out(it, peer):
        return pltpu.make_async_remote_copy(
            src_ref=sums.at[it, peer], dst_ref=before.at[it, me],
            send_sem=send_sem.at[it, 1, peer], recv_sem=recv_sem.at[it, 1, me],
            device_id={"tm": peer}, device_id_type=MESH,
        )

    def back_in(it, peer):
        return pltpu.make_async_remote_copy(
            src_ref=sums.at[it, peer], dst_ref=before.at[it, peer],
            send_sem=send_sem.at[it, 1, peer], recv_sem=recv_sem.at[it, 1, peer],
            device_id={"tm": peer}, device_id_type=MESH,
        )

    for it in range(ITERS):
        for channel in range(channels):
            for frame in range(frames):
                for part in range(halves):
                    lanes = slice(part * LANES, (part + 1) * LANES)
                    state = start_ref[channel, frame, :, lanes]
                    tile = frame * halves + part
                    if it > 0:
                        shift = [
                            before[it - 1, owner, channel, slot : slot + size, :]
                            for owner, slot, first, size in groups(tile)
                        ]
                        state = state + jnp.concatenate(shift, axis=0)
                    for row in range(rows):
                        cols[frame * rows + row, channel : channel + 1, lanes] = state[row : row + 1]
        network()
        for channel in range(channels):
            for frame in range(frames):
                for part in range(halves):
                    lanes = slice(part * LANES, (part + 1) * LANES)
                    tile = frame * halves + part
                    drift = (
                        step_size * value[channel, tile]
                        + NOISE_SCALE * math.sqrt(step_size) * noise_ref[channel, frame, :, lanes]
                    )
                    value[channel, tile] = drift
                    for owner, slot, first, size in groups(tile):
                        sent[it, owner, channel, slot : slot + size, :] = drift[first : first + size]
        if it == 0:
            pl.semaphore_wait(barrier, n - 1)

        @pl.loop(1, n)
        def _(k):
            copy_out(it, lax.rem(me + k, n)).start()

        got[it, me] = sent[it, me]

        def advance(peer, running):
            sums[it, peer] = running

            @pl.when(peer != me)
            def _():
                back_out(it, peer).start()
                copy_in(it, peer).wait_recv()

            return running + got[it, peer]

        lax.fori_loop(0, n, advance, jnp.zeros((channels, share, LANES), jnp.float32))
        before[it, me] = sums[it, me]

        @pl.loop(1, n)
        def _(k):
            peer = lax.rem(me + k, n)
            back_in(it, peer).wait_recv()
            copy_out(it, peer).wait_send()
            back_out(it, peer).wait_send()

    it = ITERS - 1
    for channel in range(channels):
        for frame in range(frames):
            for part in range(halves):
                lanes = slice(part * LANES, (part + 1) * LANES)
                tile = frame * halves + part
                shift = jnp.concatenate(
                    [
                        before[it, owner, channel, slot : slot + size, :]
                        for owner, slot, first, size in groups(tile)
                    ],
                    axis=0,
                )
                out_ref[channel, frame, :, lanes] = (
                    start_ref[channel, frame, :, lanes] + shift + value[channel, tile]
                )


def shards(start_frames, plan, noise, w_lift, w_time, spatial, temporal, w_point, w_out):
    n = lax.axis_size("tm")
    channels, frames, rows, width = start_frames.shape
    hid = w_time.shape[0]
    blocks = spatial.shape[0]
    bias = jnp.dot(embedding(plan[0], hid)[None], w_time, precision=lax.Precision.HIGHEST)
    tiles = frames * (width // LANES)
    share = -(-tiles * rows // n)
    vmem = pl.BlockSpec(memory_space=pltpu.VMEM)
    exchange = pltpu.VMEM((ITERS, n, channels, share, LANES), jnp.float32)
    features = pltpu.VMEM((frames * rows, width + 2 * HALO, hid), jnp.float32)
    result = pl.pallas_call(
        functools.partial(kernel, n, share),
        out_shape=jax.ShapeDtypeStruct(start_frames.shape, jnp.float32),
        in_specs=[vmem] * 8,
        out_specs=vmem,
        scratch_shapes=[
            features,
            features,
            pltpu.VMEM((frames * rows, 8, width), jnp.float32),
            pltpu.VMEM((32, hid), jnp.float32),
            pltpu.VMEM((16, hid), jnp.float32),
            pltpu.VMEM((blocks, 6 * hid, 2 * hid), jnp.bfloat16),
            pltpu.VMEM((blocks + 1, 2 * hid, 2 * hid), jnp.bfloat16),
            pltpu.VMEM((frames * rows // 2 * TILE_W, 2 * hid), jnp.float32),
            pltpu.VMEM((channels, tiles, rows, LANES), jnp.float32),
            exchange,
            exchange,
            exchange,
            exchange,
            pltpu.SemaphoreType.DMA((ITERS, 2, n)),
            pltpu.SemaphoreType.DMA((ITERS, 2, n)),
        ],
        compiler_params=pltpu.CompilerParams(
            collective_id=0, has_side_effects=True, vmem_limit_bytes=48 * 2**20
        ),
    )(
        start_frames, noise[0], bias, w_lift,
        spatial.transpose(2, 0, 1), temporal.transpose(2, 0, 1), w_point, w_out.T,
    )
    return result[None]


def solution(mesh):
    in_specs = (
        P("groups", None, None, None),
        P(("groups", "tm")),
        P("tm", "groups", None, None, None),
        P(),
        P(),
        P(),
        P(),
        P(),
        P(),
    )
    out_specs = P("tm", "groups", None, None, None)
    return jax.shard_map(shards, mesh=mesh, in_specs=in_specs, out_specs=out_specs, check_vma=False)
```

profile of v0, /device:TPU:25, one launch (start us, length us, event | category | flops | bytes accessed | tf_op | source)
XLA Modules:
  0.0 45.8 jit_solution(4070309772810165317)
XLA Ops:
  0.0 0.0 copy-start
  0.0 0.0 copy-start.3
  0.7 0.1 copy-done
  0.8 0.0 copy-start.4
  0.8 0.0 copy-start.5
  0.8 0.0 copy-start.6
  0.8 0.0 copy-start.7
  0.9 0.2 fusion.bias_ref
  1.1 0.0 copy-done.3
  1.1 0.5 %copy-done.4 = f32[2,128,9]{1,0,2:T(2,128)S(1)} copy-done((f32[2,128,9]{1,0,2:T(2,128)S(1)}, f32[2,128,9]{1,0,2:T(2,128)}, u32[]{:S(2)}) %copy-start.4) | copy-done | bytes 9240
  1.5 0.0 copy-done.5
  1.6 0.0 copy-done.6
  1.6 0.0 copy-done.7
  1.6 0.0 copy-start.1
  1.6 0.9 %copy-done.1 = f32[3,4,8,256]{3,2,1,0:T(8,128)S(1)} copy-done((f32[3,4,8,256]{3,2,1,0:T(8,128)S(1)}, f32[3,4,8,256]{3,2,1,0:T(8,128)}, u32[]{:S(2)}) %copy-start.1) | copy-done | bytes 98328
  2.5 0.0 copy-start.2
  2.5 0.9 %copy-done.2 = f32[1,3,4,8,256]{4,3,2,1,0:T(8,128)S(1)} copy-done((f32[1,3,4,8,256]{4,3,2,1,0:T(8,128)S(1)}, f32[1,3,4,8,256]{4,3,2,1,0:T(8,128)}, u32[]{:S(2)}) %copy-start.2) | copy-done | bytes 98328
  3.4 41.8 %shard_map.91 = f32[3,4,8,256]{3,2,1,0:T(8,128)S(1)} custom-call(f32[3,4,8,256]{3,2,1,0:T(8,128)S(1)} %copy-done.1, f32[3,4,8,256]{3,2,1,0:T(8,128)S(1)} %bitcast.12, f32[1,128]{1,0:T(1,128)S(1)} %fusion.bias_ref, f32[3,128]{1,0:T(4,128)S(1)} %copy-done.6, f32[9,2,128]{2,1,0:T(2,128)S(1)} %bitcast.13, f32[3,2,128]{2,1,0:T(2,128)S(1)} %bitcast.14, ...), custom_call_target="tpu_custom_call" | custom-call | tf_op jit(solution)/shard_map/pallas_call | solution.py:344
  45.2 0.6 %copy.12 = f32[1,3,4,8,256]{4,3,2,1,0:T(8,128)} copy(f32[1,3,4,8,256]{4,3,2,1,0:T(8,128)S(1)} %bitcast.11) | data formatting | bytes 196608
  (1 shorter events, 0.0 us)
Async XLA Ops:
  0.0 0.8 %copy-start = (f32[128,128]{1,0:T(8,128)S(1)}, f32[128,128]{1,0:T(8,128)}, u32[]{:S(2)}) copy-start(f32[128,128]{1,0:T(8,128)} %param.13) | copy-start | bytes 196612
  0.0 1.1 %copy-start.3 = (bf16[2,128,128]{2,1,0:T(8,128)(2,1)S(1)}, bf16[2,128,128]{2,1,0:T(8,128)(2,1)}, u32[]{:S(2)}) copy-start(bf16[2,128,128]{2,1,0:T(8,128)(2,1)} %point_ref.1) | copy-start | bytes 196612
  0.8 0.7 %copy-start.4 = (f32[2,128,9]{1,0,2:T(2,128)S(1)}, f32[2,128,9]{1,0,2:T(2,128)}, u32[]{:S(2)}) copy-start(f32[2,128,9]{1,0,2:T(2,128)} %param.14) | copy-start | bytes 27652
  0.8 0.7 %copy-start.5 = (f32[2,128,3]{1,0,2:T(2,128)S(1)}, f32[2,128,3]{1,0,2:T(2,128)}, u32[]{:S(2)}) copy-start(f32[2,128,3]{1,0,2:T(2,128)} %param.15) | copy-start | bytes 9220
  0.8 0.7 %copy-start.6 = (f32[3,128]{1,0:T(4,128)S(1)}, f32[3,128]{1,0:T(4,128)}, u32[]{:S(2)}) copy-start(f32[3,128]{1,0:T(4,128)} %lift_ref.1) | copy-start | bytes 4612
  0.8 0.7 %copy-start.7 = (f32[128,3]{0,1:T(4,128)S(1)}, f32[128,3]{0,1:T(4,128)}, u32[]{:S(2)}) copy-start(f32[128,3]{0,1:T(4,128)} %param.17) | copy-start | bytes 4612
  1.6 0.9 %copy-start.1 = (f32[3,4,8,256]{3,2,1,0:T(8,128)S(1)}, f32[3,4,8,256]{3,2,1,0:T(8,128)}, u32[]{:S(2)}) copy-start(f32[3,4,8,256]{3,2,1,0:T(8,128)} %start_ref.1) | copy-start | bytes 294916
  2.5 0.9 %copy-start.2 = (f32[1,3,4,8,256]{4,3,2,1,0:T(8,128)S(1)}, f32[1,3,4,8,256]{4,3,2,1,0:T(8,128)}, u32[]{:S(2)}) copy-start(f32[1,3,4,8,256]{4,3,2,1,0:T(8,128)} %param.11) | copy-start | bytes 294916
where the time goes:
time: 46.4 us; the launch traced here: 45.8 us
  Pallas kernels  41.8 us (90%)
  local copies, waits for them, and re-layouts  3.04 us (7%)
  between operations  0.71 us (2%)
    pallas_call x1, Pallas kernels, shards(): pl.pallas_call(functools.partial(kernel, n, share), out_shape=jax.ShapeDt...  41.8 us
    unnamed x17, local copies, waits for them, and re-layouts  3.04 us

commit v1 on v0

v1 whole, which is shorter than its diff:
```python
import functools
import math

import jax
import jax.numpy as jnp
from jax import lax
from jax.experimental import pallas as pl
from jax.experimental.pallas import tpu as pltpu
from jax.sharding import PartitionSpec as P

ITERS = 2
NOISE_SCALE = 2.0
MESH = pl.DeviceIdType.MESH
LANES = 128
STRIPS = 16
TILE = 16
NT = (((1,), (1,)), ((), ()))


def split_bf16(value):
    high = value.astype(jnp.bfloat16)
    return high, (value - high.astype(jnp.float32)).astype(jnp.bfloat16)


def kernel(
    n, quad, dims,
    plan_ref, start_hbm, noise_hbm, lift_hbm, time_hbm, spatial_hbm, temporal_hbm, point_hbm, wout_hbm,
    out_ref,
    start, noise, lift_in, time_in, spatial_in, temporal_in, point_in, wout_in,
    lift_w, out_w, state, sent, near, total, far, before, final,
    in_sem, send_sem, recv_sem,
    feat_a, feat_b, last, time_a, time_b, pend, normed, place, taps, point_w, mean_w, lift_b, out_b,
):
    channels, frames, rows, width, hid, blocks = dims
    halves = width // LANES
    planes = channels * frames
    strip = width // STRIPS
    cells = strip * STRIPS
    levels = n // quad
    step_size = 1.0 / n
    bf16 = jnp.bfloat16
    me = lax.axis_index("tm")
    level, member = lax.div(me, quad), lax.rem(me, quad)

    loads = [
        (start_hbm.at[:, pl.ds(half * LANES, LANES)], start.at[half]) for half in range(halves)
    ]
    loads += [(lift_hbm, lift_in), (time_hbm, time_in), (spatial_hbm, spatial_in)]
    loads += [(temporal_hbm, temporal_in), (point_hbm, point_in), (wout_hbm, wout_in)]
    loads += [
        (noise_hbm.at[:, pl.ds(half * LANES, LANES)], noise.at[half]) for half in range(halves)
    ]
    loads = [
        pltpu.make_async_copy(source, target, in_sem.at[k])
        for k, (source, target) in enumerate(loads)
    ]
    for load in loads:
        load.start()

    barrier = pltpu.get_barrier_semaphore()

    @pl.loop(1, n)
    def _(k):
        pl.semaphore_signal(
            barrier, inc=1, device_id={"tm": lax.rem(me + k, n)}, device_id_type=MESH
        )

    for feat in (time_a, time_b):
        for frame in range(frames):
            for row in (0, rows + 1):
                feat[frame, row] = jnp.zeros((strip + 2, STRIPS, hid), bf16)
    spot = lax.broadcasted_iota(jnp.int32, ((strip + 2) * STRIPS, width), 0)
    column = lax.broadcasted_iota(jnp.int32, ((strip + 2) * STRIPS, width), 1)
    wanted = lax.rem(spot, STRIPS) * strip + lax.div(spot, STRIPS) - 1
    place[...] = jnp.where(column == wanted, 1.0, 0.0).astype(bf16)
    one_row = lax.broadcasted_iota(jnp.int32, (rows, TILE, width), 1) == planes
    state[...] = jnp.where(one_row, 1.0, 0.0)
    lift_w[...] = jnp.zeros_like(lift_w)
    out_w[...] = jnp.zeros_like(out_w)
    mean_w[...] = jnp.zeros_like(mean_w)
    point_w[...] = jnp.zeros_like(point_w)
    for out in range(2):
        here = slice(out * hid, (out + 1) * hid)
        mean_w[here, here] = jnp.full((hid, hid), 4.0 / hid, bf16)

    lane = lax.broadcasted_iota(jnp.int32, (8, hid), 1)
    half_hid = hid // 2
    index = lax.rem(lane, half_hid).astype(jnp.float32)
    angles = plan_ref[0].astype(jnp.float32) * jnp.exp(-math.log(1000.0) * index / half_hid)
    embedded = jnp.where(lane < half_hid, jnp.sin(angles), jnp.cos(angles))

    for load in loads:
        load.wait()

    bias = jnp.dot(
        embedded, time_in[...], precision=lax.Precision.HIGHEST, preferred_element_type=jnp.float32
    )[0:1]

    def split_rows(rows_value):
        high = rows_value.astype(bf16).astype(jnp.float32)
        return high, rows_value - high

    bias_high, bias_low = split_rows(bias)
    lift_high, lift_low = split_rows(lift_in[...])
    out_high, out_low = split_rows(wout_in[...])
    for frame in range(frames):
        here = slice(frame * hid, (frame + 1) * hid)
        for channel in range(channels):
            k = channel * frames + frame
            lift_w[k : k + 1, here] = lift_high[channel : channel + 1]
            lift_w[TILE + k : TILE + k + 1, here] = lift_high[channel : channel + 1]
            lift_w[2 * TILE + k : 2 * TILE + k + 1, here] = lift_low[channel : channel + 1]
            out_w[k : k + 1, here] = out_high[channel : channel + 1]
            out_w[TILE + k : TILE + k + 1, here] = out_low[channel : channel + 1]
        lift_w[planes : planes + 1, here] = bias_high
        lift_w[2 * TILE + planes : 2 * TILE + planes + 1, here] = bias_low
    lift_b[...] = lift_w[...].astype(bf16)
    out_b[...] = out_w[...].astype(bf16)
    for block in range(blocks):
        for out in range(2):
            here = slice(out * hid, (out + 1) * hid)
            point_w[block, here, here] = point_in[block]
        for k in range(9):
            weight = spatial_in[k, block : block + 1, :]
            taps[block, k] = jnp.broadcast_to(weight, (STRIPS, hid)).astype(bf16)
        for k in range(3):
            weight = temporal_in[k, block : block + 1, :]
            taps[block, 9 + k] = jnp.broadcast_to(weight, (STRIPS, hid)).astype(bf16)

    def quad_copy(it, row, k):
        return pltpu.make_async_remote_copy(
            src_ref=sent.at[it, row], dst_ref=near.at[it, row, member],
            send_sem=send_sem.at[it, row, k], recv_sem=recv_sem.at[it, row, member],
            device_id={"tm": level * quad + lax.rem(member + k, quad)}, device_id_type=MESH,
        )

    def quad_from(it, row, k):
        other = lax.rem(member + k, quad)
        return pltpu.make_async_remote_copy(
            src_ref=sent.at[it, row], dst_ref=near.at[it, row, other],
            send_sem=send_sem.at[it, row, k], recv_sem=recv_sem.at[it, row, other],
            device_id={"tm": level * quad + other}, device_id_type=MESH,
        )

    def level_copy(it, row, k):
        return pltpu.make_async_remote_copy(
            src_ref=total.at[it, row], dst_ref=far.at[it, row, level],
            send_sem=send_sem.at[it, row, quad + k], recv_sem=recv_sem.at[it, row, quad + level],
            device_id={"tm": me + k * quad}, device_id_type=MESH,
        )

    def level_from(it, row, lower):
        return pltpu.make_async_remote_copy(
            src_ref=total.at[it, row], dst_ref=far.at[it, row, lower],
            send_sem=send_sem.at[it, row, quad], recv_sem=recv_sem.at[it, row, quad + lower],
            device_id={"tm": lower * quad + member}, device_id_type=MESH,
        )

    def send(it, row):
        @pl.loop(1, quad)
        def _(k):
            quad_copy(it, row, k).start()

    def forward(it, row):
        near[it, row, member] = sent[it, row]

        @pl.loop(1, quad)
        def _(k):
            quad_from(it, row, k).wait_recv()

        zero = jnp.zeros((halves * planes, LANES), jnp.float32)
        everything, prefix = zero, zero
        for k in range(quad):
            part = near[it, row, k]
            everything = everything + part
            prefix = prefix + jnp.where(k < member, part, 0.0)
        total[it, row] = everything
        before[it, row] = prefix

        @pl.loop(1, levels - level)
        def _(k):
            level_copy(it, row, k).start()

    def arrive(it, row):
        @pl.loop(0, level)
        def _(lower):
            level_from(it, row, lower).wait_recv()
            before[it, row] += far[it, row, lower]

    def lift(it, row, target, at_row, blend, to_row):
        for half in range(halves):
            now = start[half, pl.ds(row, planes, stride=rows), :]
            if it > 0:
                now = now + before[it - 1, row, half * planes : (half + 1) * planes]
            state[row, 0:planes, half * LANES : (half + 1) * LANES] = now
        high, low = split_bf16(state[row])
        spare = jnp.zeros((LANES - 3 * TILE, width), bf16)
        stack = jnp.concatenate([high, low, high, spare], axis=0)
        turned = lax.dot_general(place[...], stack, NT, preferred_element_type=jnp.float32)
        lifted = jnp.dot(
            turned.astype(bf16), lift_b[...], preferred_element_type=jnp.float32
        ).astype(bf16)
        fresh = [
            lifted[:, frame * hid : (frame + 1) * hid].reshape(strip + 2, STRIPS, hid)
            for frame in range(frames)
        ]
        for frame in range(frames):
            target[frame, at_row] = fresh[frame][1 : strip + 1]
            blend[frame, to_row] = in_time(fresh, frame, 0)

    def in_time(fresh, frame, block):
        mixed = taps[block, 10] * fresh[frame]
        if frame > 0:
            mixed = mixed + taps[block, 9] * fresh[frame - 1]
        if frame + 1 < frames:
            mixed = mixed + taps[block, 11] * fresh[frame + 1]
        return mixed

    def convolve(source, first, block):
        weights = [taps[block, k] for k in range(9)]
        for frame in range(frames):
            for at in range(strip):
                lines = []
                for a in range(3):
                    terms = [weights[3 * a + c] * source[frame, first + a, at + c] for c in range(3)]
                    lines.append(terms[0] + terms[1] + terms[2])
                pend[frame, at] = lines[0] + lines[1] + lines[2]

    def pairs(ref):
        return jnp.concatenate(
            [
                jnp.concatenate([ref[pair + k].reshape(cells, hid) for k in range(2)], axis=1)
                for pair in range(0, frames, 2)
            ],
            axis=0,
        )

    def normalize():
        mixed = pairs(pend)
        mean = jnp.dot(mixed * mixed, mean_w[...], preferred_element_type=jnp.float32)
        scale = lax.rsqrt(mean.astype(bf16) + jnp.bfloat16(4e-06))
        half = mixed * scale
        done = half * jnp.tanh(half) + half
        for frame in range(frames):
            first, side = (frame // 2) * cells, (frame % 2) * hid
            part = done[first : first + cells, side : side + hid]
            normed[frame] = part.reshape(strip, STRIPS, hid)

    def update(source, at_row, target, to_row, block, blend=None, blend_row=None):
        sub = lax.broadcasted_iota(jnp.int32, (STRIPS, hid), 0)
        change = jnp.dot(pairs(normed), point_w[block], preferred_element_type=jnp.float32)
        fresh = []
        for frame in range(frames):
            first, side = (frame // 2) * cells, (frame % 2) * hid
            old = source[frame, at_row].reshape(cells, hid)
            now = old + change[first : first + cells, side : side + hid].astype(bf16)
            fresh.append(now.reshape(strip, STRIPS, hid))
            target[frame, to_row] = fresh[frame]
        if blend is None:
            return
        for frame in range(frames):
            mixed = in_time(fresh, frame, block + 1)
            blend[frame, blend_row, 1 : strip + 1] = mixed
            tail = mixed[strip - 1].astype(jnp.float32)
            tail = jnp.where(sub == 0, 0.0, pltpu.roll(tail, 1, 0))
            blend[frame, blend_row, 0] = tail.astype(bf16)
            head = mixed[0].astype(jnp.float32)
            head = jnp.where(sub == STRIPS - 1, 0.0, pltpu.roll(head, STRIPS - 1, 0))
            blend[frame, blend_row, strip + 1] = head.astype(bf16)

    def output(it, row, source, at_row):
        seen = jnp.concatenate(
            [source[frame, at_row].reshape(cells, hid) for frame in range(frames)], axis=1
        )
        both = lax.dot_general(out_b[...], seen, NT, preferred_element_type=jnp.float32)
        high, low = split_bf16(both[0:TILE] + both[TILE : 2 * TILE])
        turned = jnp.dot(
            jnp.concatenate([high, low], axis=0), place[STRIPS : STRIPS + cells, :],
            preferred_element_type=jnp.float32,
        )
        turned = turned[0:TILE] + turned[TILE : 2 * TILE]
        for half in range(halves):
            drift = (
                step_size * turned[0:planes, half * LANES : (half + 1) * LANES]
                + NOISE_SCALE
                * math.sqrt(step_size)
                * noise[half, pl.ds(row, planes, stride=rows), :]
            )
            sent[it, row, half * planes : (half + 1) * planes] = drift

    def step(it, v):
        if 0 <= v - 3 - rows < rows:
            output(it, v - 3 - rows, last, v - 3 - rows)
        if 0 <= v - 2 < rows:
            update(feat_a, v - 2, feat_b, v - 2, 0, time_b, v - 1)
        elif rows <= v - 2 < 2 * rows:
            update(feat_b, v - 2 - rows, last, v - 2 - rows, 1)
        if 0 <= v - 1 < 2 * rows:
            normalize()
        if v < rows:
            convolve(time_a, v, 0)
        elif v < 2 * rows:
            convolve(time_b, v - rows, 1)
        if v + 2 < rows:
            lift(it, v + 2, feat_a, v + 2, time_a, v + 3)

    for it in range(ITERS):
        for row in range(2):
            if it > 0:
                arrive(it - 1, row)
            lift(it, row, feat_a, row, time_a, row + 1)
        for v in range(2):
            if it > 0:
                arrive(it - 1, v + 2)
            step(it, v)

        @pl.loop(2, rows - 2)
        def _(v):
            if it > 0:
                arrive(it - 1, v + 2)
            plain = feat_a.at[:, pl.ds(v - 2, 5)]
            mixed = time_a.at[:, pl.ds(v, 4)]
            update(plain, 0, feat_b.at[:, pl.ds(v - 2, 1)], 0, 0, time_b.at[:, pl.ds(v - 1, 1)], 0)
            normalize()
            convolve(mixed, 0, 0)
            lift(it, v + 2, plain, 4, mixed, 3)

        for v in range(rows - 2, rows + 3):
            step(it, v)
        if it == 0:
            pl.semaphore_wait(barrier, n - 1)

        @pl.loop(rows + 3, 2 * rows)
        def _(v):
            row = v - rows
            seen = last.at[:, pl.ds(row - 3, 2)]
            output(it, row - 3, seen, 0)
            update(feat_b.at[:, pl.ds(row - 2, 1)], 0, seen, 1, 1)
            normalize()
            convolve(time_b.at[:, pl.ds(row, 3)], 0, 1)
            send(it, row - 3)

        for v in range(2 * rows, 2 * rows + 3):
            step(it, v)
            send(it, v - 3 - rows)
            forward(it, v - 2 * rows)

        @pl.loop(3, rows)
        def _(row):
            forward(it, row)

    it = ITERS - 1

    @pl.loop(0, rows)
    def _(row):
        arrive(it, row)
        done = before[it, row] + sent[it, row]
        for half in range(halves):
            here_rows = pl.ds(row, planes, stride=rows)
            final[half, here_rows, :] = (
                start[half, here_rows, :] + done[half * planes : (half + 1) * planes]
            )

    for half in range(halves):
        out_ref[:, half * LANES : (half + 1) * LANES] = final[half]

    for it in range(ITERS):
        @pl.loop(0, rows)
        def _(row):
            @pl.loop(1, quad)
            def _(k):
                quad_copy(it, row, k).wait_send()

            @pl.loop(1, levels - level)
            def _(k):
                level_copy(it, row, k).wait_send()


def scoped(n, quad, dims, *refs):
    channels, frames, rows, width, hid, blocks = dims
    strip = width // STRIPS
    packed = lambda *shape: pltpu.VMEM(shape, jnp.bfloat16)
    pl.run_scoped(
        functools.partial(kernel, n, quad, dims, *refs),
        packed(frames, rows, strip, STRIPS, hid),
        packed(frames, rows, strip, STRIPS, hid),
        packed(frames, rows, strip, STRIPS, hid),
        packed(frames, rows + 2, strip + 2, STRIPS, hid),
        packed(frames, rows + 2, strip + 2, STRIPS, hid),
        packed(frames, strip, STRIPS, hid),
        packed(frames, strip, STRIPS, hid),
        packed((strip + 2) * STRIPS, width),
        packed(blocks, 12, STRIPS, hid),
        packed(blocks, 2 * hid, 2 * hid),
        packed(2 * hid, 2 * hid),
        packed(LANES, frames * hid),
        packed(2 * TILE, frames * hid),
    )


def shards(start_frames, plan, noise, w_lift, w_time, spatial, temporal, w_point, w_out):
    n = lax.axis_size("tm")
    channels, frames, rows, width = start_frames.shape
    hid = w_time.shape[0]
    blocks = spatial.shape[0]
    halves = width // LANES
    planes = channels * frames
    quad = max(k for k in range(1, n + 1) if n % k == 0 and k * k <= n)
    flat = (planes * rows, width)
    hbm = pl.BlockSpec(memory_space=pl.ANY)
    f32, bf16 = jnp.float32, jnp.bfloat16
    line = pltpu.VMEM((ITERS, rows, halves * planes, LANES), f32)
    by_half = pltpu.VMEM((halves, planes * rows, LANES), f32)
    result = pl.pallas_call(
        functools.partial(scoped, n, quad, (channels, frames, rows, width, hid, blocks)),
        out_shape=jax.ShapeDtypeStruct(flat, f32),
        in_specs=[pl.BlockSpec(memory_space=pltpu.SMEM)] + [hbm] * 8,
        out_specs=pl.BlockSpec(memory_space=pltpu.VMEM),
        scratch_shapes=[
            by_half,
            by_half,
            pltpu.VMEM((channels, hid), f32),
            pltpu.VMEM((hid, hid), f32),
            pltpu.VMEM((9, blocks, hid), f32),
            pltpu.VMEM((3, blocks, hid), f32),
            pltpu.VMEM((blocks, hid, hid), bf16),
            pltpu.VMEM((channels, hid), f32),
            pltpu.VMEM((LANES, frames * hid), f32),
            pltpu.VMEM((2 * TILE, frames * hid), f32),
            pltpu.VMEM((rows, TILE, width), f32),
            line,
            pltpu.VMEM((ITERS, rows, quad, halves * planes, LANES), f32),
            line,
            pltpu.VMEM((ITERS, rows, n // quad, halves * planes, LANES), f32),
            line,
            by_half,
            pltpu.SemaphoreType.DMA((2 * halves + 6,)),
            pltpu.SemaphoreType.DMA((ITERS, rows, quad + n // quad)),
            pltpu.SemaphoreType.DMA((ITERS, rows, quad + n // quad)),
        ],
        compiler_params=pltpu.CompilerParams(
            collective_id=0, has_side_effects=True, vmem_limit_bytes=62 * 2**20
        ),
    )(
        plan, start_frames.reshape(flat), noise.reshape(flat), w_lift, w_time,
        spatial.transpose(2, 0, 1), temporal.transpose(2, 0, 1), w_point, w_out.T,
    )
    return result.reshape((1,) + start_frames.shape)


def solution(mesh):
    in_specs = (
        P("groups", None, None, None),
        P(("groups", "tm")),
        P("tm", "groups", None, None, None),
        P(),
        P(),
        P(),
        P(),
        P(),
        P(),
    )
    out_specs = P("tm", "groups", None, None, None)
    return jax.shard_map(shards, mesh=mesh, in_specs=in_specs, out_specs=out_specs, check_vma=False)
```

time: 46.4 us -> 39.6 us (0.85)
  Pallas kernels: 41.8 us -> 37.2 us
  local copies, waits for them, and re-layouts: 3.04 us -> 1.54 us
    pallas_call x1, Pallas kernels: 41.8 us -> 37.2 us  [shards(): pl.pallas_call(functools.partial(scoped, n, quad, (channels, frames, rows...]
    unnamed x17 -> x1, local copies, waits for them, and re-layouts: 3.04 us -> 1.54 us
where the time goes in v1:
time: 39.6 us; the launch traced here: 39.4 us
  Pallas kernels  37.2 us (94%)
  local copies, waits for them, and re-layouts  1.54 us (4%)
  between operations  0.66 us (2%)
    pallas_call x1, Pallas kernels, shards(): pl.pallas_call(functools.partial(scoped, n, quad, (channels, frames, rows...  37.2 us
    unnamed x1, local copies, waits for them, and re-layouts  1.54 us

profile of v1, /device:TPU:25, one launch (start us, length us, event | category | flops | bytes accessed | tf_op | source)
XLA Modules:
  0.0 39.4 jit_solution(5133329027636899152)
XLA Ops:
  0.7 37.2 %shard_map.91 = f32[96,256]{1,0:T(8,128)} custom-call(s32[1]{0:T(128)S(6)} %copy.11.refs_0_, f32[96,256]{1,0:T(8,128)} %bitcast.7, f32[96,256]{1,0:T(8,128)} %bitcast.8, f32[3,128]{1,0:T(4,128)} %refs_3_.1, f32[128,128]{1,0:T(8,128)} %refs_4_.1, f32[9,2,128]{2,1,0:T(2,128)} %bitcast.9, f32[3,2,128]{2,1,0:T(2,128)} %bitcast.10, bf16[2,128,128]{2,1,0:T(8,128)(2,1)} %refs_7_.1, ...), custom_call_target="tpu_custom_call" | custom-call | tf_op jit(solution)/shard_map/pallas_call | solution.py:414
  37.9 1.5 %copy.12 = f32[1,3,4,8,256]{4,3,2,1,0:T(8,128)} copy(f32[1,3,4,8,256]{4,3,2,1,0:T(8,128)} %bitcast.6) | data formatting | bytes 196608

commit v2 on v1

--- a/solution.py
+++ b/solution.py
@@ -14,6 +14,7 @@
 LANES = 128
 STRIPS = 16
 TILE = 16
+WAIT = 5
 NT = (((1,), (1,)), ((), ()))
 
 
@@ -27,7 +28,7 @@
     plan_ref, start_hbm, noise_hbm, lift_hbm, time_hbm, spatial_hbm, temporal_hbm, point_hbm, wout_hbm,
     out_ref,
     start, noise, lift_in, time_in, spatial_in, temporal_in, point_in, wout_in,
-    lift_w, out_w, state, sent, near, total, far, before, final,
+    lift_w, out_w, state, near, far, before, final,
     in_sem, send_sem, recv_sem,
     feat_a, feat_b, last, time_a, time_b, pend, normed, place, taps, point_w, mean_w, lift_b, out_b,
 ):
@@ -129,52 +130,53 @@
 
     def quad_copy(it, row, k):
         return pltpu.make_async_remote_copy(
-            src_ref=sent.at[it, row], dst_ref=near.at[it, row, member],
-            send_sem=send_sem.at[it, row, k], recv_sem=recv_sem.at[it, row, member],
+            src_ref=near.at[it, row, member], dst_ref=near.at[it, row, member],
+            send_sem=send_sem.at[k - 1], recv_sem=recv_sem.at[it, row, 0],
             device_id={"tm": level * quad + lax.rem(member + k, quad)}, device_id_type=MESH,
-        )
-
-    def quad_from(it, row, k):
-        other = lax.rem(member + k, quad)
-        return pltpu.make_async_remote_copy(
-            src_ref=sent.at[it, row], dst_ref=near.at[it, row, other],
-            send_sem=send_sem.at[it, row, k], recv_sem=recv_sem.at[it, row, other],
-            device_id={"tm": level * quad + other}, device_id_type=MESH,
         )
 
     def level_copy(it, row, k):
         return pltpu.make_async_remote_copy(
-            src_ref=total.at[it, row], dst_ref=far.at[it, row, level],
-            send_sem=send_sem.at[it, row, quad + k], recv_sem=recv_sem.at[it, row, quad + level],
+            src_ref=far.at[it, row, level], dst_ref=far.at[it, row, level],
+            send_sem=send_sem.at[quad + k - 2], recv_sem=recv_sem.at[it, row, 1 + level],
             device_id={"tm": me + k * quad}, device_id_type=MESH,
         )
 
     def level_from(it, row, lower):
         return pltpu.make_async_remote_copy(
-            src_ref=total.at[it, row], dst_ref=far.at[it, row, lower],
-            send_sem=send_sem.at[it, row, quad], recv_sem=recv_sem.at[it, row, quad + lower],
+            src_ref=far.at[it, row, lower], dst_ref=far.at[it, row, lower],
+            send_sem=send_sem.at[0], recv_sem=recv_sem.at[it, row, 1 + lower],
             device_id={"tm": lower * quad + member}, device_id_type=MESH,
         )
 
+    def quad_from(it, row):
+        others = pl.ds(0, quad - 1)
+        return pltpu.make_async_remote_copy(
+            src_ref=near.at[it, row, others], dst_ref=near.at[it, row, others],
+            send_sem=send_sem.at[0], recv_sem=recv_sem.at[it, row, 0],
+            device_id={"tm": me}, device_id_type=MESH,
+        )
+
+    def all_sent(ref, k):
+        return pltpu.make_async_remote_copy(
+            src_ref=ref.at[:, :, 0], dst_ref=ref.at[:, :, 0],
+            send_sem=send_sem.at[k], recv_sem=recv_sem.at[0, 0, 0],
+            device_id={"tm": me}, device_id_type=MESH,
+        )
+
     def send(it, row):
-        @pl.loop(1, quad)
-        def _(k):
+        for k in range(1, quad):
             quad_copy(it, row, k).start()
 
     def forward(it, row):
-        near[it, row, member] = sent[it, row]
-
-        @pl.loop(1, quad)
-        def _(k):
-            quad_from(it, row, k).wait_recv()
-
+        quad_from(it, row).wait_recv()
         zero = jnp.zeros((halves * planes, LANES), jnp.float32)
         everything, prefix = zero, zero
         for k in range(quad):
             part = near[it, row, k]
             everything = everything + part
             prefix = prefix + jnp.where(k < member, part, 0.0)
-        total[it, row] = everything
+        far[it, row, level] = everything
         before[it, row] = prefix
 
         @pl.loop(1, levels - level)
@@ -286,7 +288,7 @@
                 * math.sqrt(step_size)
                 * noise[half, pl.ds(row, planes, stride=rows), :]
             )
-            sent[it, row, half * planes : (half + 1) * planes] = drift
+            near[it, row, member, half * planes : (half + 1) * planes] = drift
 
     def step(it, v):
         if 0 <= v - 3 - rows < rows:
@@ -309,71 +311,40 @@
             if it > 0:
                 arrive(it - 1, row)
             lift(it, row, feat_a, row, time_a, row + 1)
-        for v in range(2):
-            if it > 0:
+        for v in range(2 * rows + 3):
+            if it > 0 and v + 2 < rows:
                 arrive(it - 1, v + 2)
             step(it, v)
-
-        @pl.loop(2, rows - 2)
-        def _(v):
-            if it > 0:
-                arrive(it - 1, v + 2)
-            plain = feat_a.at[:, pl.ds(v - 2, 5)]
-            mixed = time_a.at[:, pl.ds(v, 4)]
-            update(plain, 0, feat_b.at[:, pl.ds(v - 2, 1)], 0, 0, time_b.at[:, pl.ds(v - 1, 1)], 0)
-            normalize()
-            convolve(mixed, 0, 0)
-            lift(it, v + 2, plain, 4, mixed, 3)
-
-        for v in range(rows - 2, rows + 3):
-            step(it, v)
-        if it == 0:
-            pl.semaphore_wait(barrier, n - 1)
-
-        @pl.loop(rows + 3, 2 * rows)
-        def _(v):
-            row = v - rows
-            seen = last.at[:, pl.ds(row - 3, 2)]
-            output(it, row - 3, seen, 0)
-            update(feat_b.at[:, pl.ds(row - 2, 1)], 0, seen, 1, 1)
-            normalize()
-            convolve(time_b.at[:, pl.ds(row, 3)], 0, 1)
-            send(it, row - 3)
-
-        for v in range(2 * rows, 2 * rows + 3):
-            step(it, v)
-            send(it, v - 3 - rows)
-            forward(it, v - 2 * rows)
-
-        @pl.loop(3, rows)
-        def _(row):
+            done = v - 3 - rows
+            if done < 0:
+                continue
+            if it == 0 and done == 0:
+                pl.semaphore_wait(barrier, n - 1)
+            send(it, done)
+            if done >= WAIT:
+                forward(it, done - WAIT)
+        for row in range(rows - WAIT, rows):
             forward(it, row)
 
     it = ITERS - 1
 
-    @pl.loop(0, rows)
-    def _(row):
+    for row in range(rows):
         arrive(it, row)
-        done = before[it, row] + sent[it, row]
+        done = before[it, row] + near[it, row, member]
         for half in range(halves):
-            here_rows = pl.ds(row, planes, stride=rows)
-            final[half, here_rows, :] = (
-                start[half, here_rows, :] + done[half * planes : (half + 1) * planes]
+            places = pl.ds(row, planes, stride=rows)
+            final[half, places, :] = (
+                start[half, places, :] + done[half * planes : (half + 1) * planes]
             )
-
     for half in range(halves):
         out_ref[:, half * LANES : (half + 1) * LANES] = final[half]
 
-    for it in range(ITERS):
-        @pl.loop(0, rows)
-        def _(row):
-            @pl.loop(1, quad)
-            def _(k):
-                quad_copy(it, row, k).wait_send()
-
-            @pl.loop(1, levels - level)
-            def _(k):
-                level_copy(it, row, k).wait_send()
+    for k in range(quad - 1):
+        all_sent(near, k).wait_send()
+
+    @pl.loop(1, levels - level)
+    def _(k):
+        all_sent(far, quad + k - 2).wait_send()
 
 
 def scoped(n, quad, dims, *refs):
@@ -409,7 +380,6 @@
     flat = (planes * rows, width)
     hbm = pl.BlockSpec(memory_space=pl.ANY)
     f32, bf16 = jnp.float32, jnp.bfloat16
-    line = pltpu.VMEM((ITERS, rows, halves * planes, LANES), f32)
     by_half = pltpu.VMEM((halves, planes * rows, LANES), f32)
     result = pl.pallas_call(
         functools.partial(scoped, n, quad, (channels, frames, rows, width, hid, blocks)),
@@ -428,15 +398,13 @@
             pltpu.VMEM((LANES, frames * hid), f32),
             pltpu.VMEM((2 * TILE, frames * hid), f32),
             pltpu.VMEM((rows, TILE, width), f32),
-            line,
             pltpu.VMEM((ITERS, rows, quad, halves * planes, LANES), f32),
-            line,
             pltpu.VMEM((ITERS, rows, n // quad, halves * planes, LANES), f32),
-            line,
+            pltpu.VMEM((ITERS, rows, halves * planes, LANES), f32),
             by_half,
             pltpu.SemaphoreType.DMA((2 * halves + 6,)),
-            pltpu.SemaphoreType.DMA((ITERS, rows, quad + n // quad)),
-            pltpu.SemaphoreType.DMA((ITERS, rows, quad + n // quad)),
+            pltpu.SemaphoreType.DMA((quad + n // quad - 2,)),
+            pltpu.SemaphoreType.DMA((ITERS, rows, n // quad)),
         ],
         compiler_params=pltpu.CompilerParams(
             collective_id=0, has_side_effects=True, vmem_limit_bytes=62 * 2**20

time: 39.6 us -> 36 us (0.909)
  Pallas kernels: 37.2 us -> 33.6 us
    pallas_call x1, Pallas kernels: 37.2 us -> 33.6 us  [shards(): pl.pallas_call(functools.partial(scoped, n, quad, (channels, frames, rows...]
where the time goes in v2:
time: 36 us; the launch traced here: 35.8 us
  Pallas kernels  33.6 us (93%)
  local copies, waits for them, and re-layouts  1.54 us (4%)
  between operations  0.66 us (2%)
    pallas_call x1, Pallas kernels, shards(): pl.pallas_call(functools.partial(scoped, n, quad, (channels, frames, rows...  33.6 us
    unnamed x1, local copies, waits for them, and re-layouts  1.54 us

profile of v2, /device:TPU:25, one launch (start us, length us, event | category | flops | bytes accessed | tf_op | source)
XLA Modules:
  0.0 35.8 jit_solution(14621023140127231873)
XLA Ops:
  0.7 33.6 %shard_map.91 = f32[96,256]{1,0:T(8,128)} custom-call(s32[1]{0:T(128)S(6)} %copy.11.refs_0_, f32[96,256]{1,0:T(8,128)} %bitcast.7, f32[96,256]{1,0:T(8,128)} %bitcast.8, f32[3,128]{1,0:T(4,128)} %refs_3_.1, f32[128,128]{1,0:T(8,128)} %refs_4_.1, f32[9,2,128]{2,1,0:T(2,128)} %bitcast.9, f32[3,2,128]{2,1,0:T(2,128)} %bitcast.10, bf16[2,128,128]{2,1,0:T(8,128)(2,1)} %refs_7_.1, ...), custom_call_target="tpu_custom_call" | custom-call | tf_op jit(solution)/shard_map/pallas_call | solution.py:384
  34.3 1.5 %copy.12 = f32[1,3,4,8,256]{4,3,2,1,0:T(8,128)} copy(f32[1,3,4,8,256]{4,3,2,1,0:T(8,128)} %bitcast.6) | data formatting | bytes 196608

commit v3 on v2

--- a/solution.py
+++ b/solution.py
@@ -307,6 +307,7 @@
             lift(it, v + 2, feat_a, v + 2, time_a, v + 3)
 
     for it in range(ITERS):
+        wait = WAIT if it + 1 < ITERS else rows
         for row in range(2):
             if it > 0:
                 arrive(it - 1, row)
@@ -321,9 +322,9 @@
             if it == 0 and done == 0:
                 pl.semaphore_wait(barrier, n - 1)
             send(it, done)
-            if done >= WAIT:
-                forward(it, done - WAIT)
-        for row in range(rows - WAIT, rows):
+            if done >= wait:
+                forward(it, done - wait)
+        for row in range(rows - wait, rows):
             forward(it, row)
 
     it = ITERS - 1

time: 36 us -> 36.7 us (1.019)
  Pallas kernels: 33.6 us -> 34.3 us
    pallas_call x1, Pallas kernels: 33.6 us -> 34.3 us  [shards(): pl.pallas_call(functools.partial(scoped, n, quad, (channels, frames, rows...]
where the time goes in v3:
time: 36.7 us; the launch traced here: 36.5 us
  Pallas kernels  34.3 us (93%)
  local copies, waits for them, and re-layouts  1.54 us (4%)
  between operations  0.66 us (2%)
    pallas_call x1, Pallas kernels, shards(): pl.pallas_call(functools.partial(scoped, n, quad, (channels, frames, rows...  34.3 us
    unnamed x1, local copies, waits for them, and re-layouts  1.54 us

profile of v3, /device:TPU:25, one launch (start us, length us, event | category | flops | bytes accessed | tf_op | source)
XLA Modules:
  0.0 36.5 jit_solution(14954884263504797433)
XLA Ops:
  0.7 34.3 %shard_map.91 = f32[96,256]{1,0:T(8,128)} custom-call(s32[1]{0:T(128)S(6)} %copy.11.refs_0_, f32[96,256]{1,0:T(8,128)} %bitcast.7, f32[96,256]{1,0:T(8,128)} %bitcast.8, f32[3,128]{1,0:T(4,128)} %refs_3_.1, f32[128,128]{1,0:T(8,128)} %refs_4_.1, f32[9,2,128]{2,1,0:T(2,128)} %bitcast.9, f32[3,2,128]{2,1,0:T(2,128)} %bitcast.10, bf16[2,128,128]{2,1,0:T(8,128)(2,1)} %refs_7_.1, ...), custom_call_target="tpu_custom_call" | custom-call | tf_op jit(solution)/shard_map/pallas_call | solution.py:385
  34.9 1.5 %copy.12 = f32[1,3,4,8,256]{4,3,2,1,0:T(8,128)} copy(f32[1,3,4,8,256]{4,3,2,1,0:T(8,128)} %bitcast.6) | data formatting | bytes 196608
